TPU v7x, 256 devices: a whole 4x4x8 slice. The times are simulated.
256 devices in a mesh: dp: 32 (over x, y, z_lo), cent: 8 (over z_hi, core).
Axes of the slice: x: 4, y: 4, z: 8 (z_hi: 4, z_lo: 2; z = z_hi * 2 + z_lo), core: 2. Of those that a mesh axis runs over, the one named last changes fastest.
Arguments:
- points: bfloat16 [32768, 256], P('dp'), may hold values from -8 to 8
- centroids: bfloat16 [32768, 256], P('cent'), may hold values from -0.5 to 0.5
Outputs:
- new_centroids: float32 [32768, 256], P('cent')
- counts: float32 [32768], P('cent')
- log_evidence: float32 [32768], P('dp')
All inputs are finite; a program needn't handle non-finite values.
Results may differ from a plain program's by a relative error of at most 0.0016.
Values sent between devices are 32-bit elements; how exact they have to be, the bound alone decides.
A program may use at most 64 MiB of HBM per device.

v0:
```python
import math
import jax
import jax.numpy as jnp
from jax import lax
from jax.sharding import PartitionSpec as P

prior_mass = 0.5


def body(points, centroids):
    rows = points.shape[0]
    local_cent = centroids.shape[0]
    width = centroids.shape[1]
    every_centroid = local_cent * lax.axis_size("cent")
    block = min(512, rows)
    cnorm = jnp.einsum("kd,kd->k", centroids, centroids, preferred_element_type=jnp.float32)
    sums = jnp.zeros((local_cent, width), jnp.float32)
    counts = jnp.zeros((local_cent,), jnp.float32)
    evidence = []
    for step in range(rows // block):
        piece = lax.slice_in_dim(points, step * block, (step + 1) * block, axis=0)
        dots = jnp.einsum("nd,kd->nk", piece, centroids, preferred_element_type=jnp.float32)
        score = 2.0 * dots - cnorm[None, :]
        top = lax.pmax(jnp.max(score, axis=1), "cent")
        weights = jnp.exp(score - top[:, None])
        total = lax.psum(jnp.sum(weights, axis=1), "cent")
        resp = (weights / total[:, None]).astype(jnp.bfloat16)
        sums = sums + jnp.einsum("nk,nd->kd", resp, piece, preferred_element_type=jnp.float32)
        counts = counts + jnp.sum(resp.astype(jnp.float32), axis=0)
        evidence.append(top + jnp.log(total) - math.log(every_centroid))
    log_evidence = jnp.concatenate(evidence, axis=0)
    all_sums, all_counts = lax.psum((sums, counts), "dp")
    new_centroids = (all_sums + prior_mass * centroids.astype(jnp.float32)) / (
        all_counts + prior_mass
    )[:, None]
    return (new_centroids, all_counts, log_evidence)


def solution(mesh):
    return jax.shard_map(
        body,
        mesh=mesh,
        in_specs=(P("dp", None), P("cent", None)),
        out_specs=(P("cent", None), P("cent"), P("dp")),
        check_vma=False,
    )
```

profile of v0, /device:TPU:64, one launch (start us, length us, event | category | flops | bytes accessed | tf_op | source)
XLA Modules:
  0.0 424.3 jit_solution(17040239577599494853)
XLA Ops:
  7.2 0.0 copy-start.1
  7.2 0.0 copy-start.2
  7.2 0.0 all-reduce.4.cloned.1.call-start
  7.2 2.4 fusion.4
  9.6 3.0 fusion.12
  12.6 0.0 copy-done.1
  12.6 0.0 copy-done.2
  12.6 0.0 copy-start
  12.6 4.9 %fusion.1 = (f32[512]{0:T(512)S(1)}, f32[512]{0:T(512)S(1)}, f32[512,4096]{1,0:T(8,128)}) fusion(f32[4096]{0:T(1024)S(1)} %fusion.4, f32[512,4096]{1,0:T(8,128)S(1)} %fusion.12, bf16[4096,256]{1,0:T(8,128)(2,1)S(1)} %copy-done.1, bf16[1024,256]{1,0:T(8,128)(2,1)S(1)} %copy-done.2), kind=kOutput, calls=%fused_computation.9 | convolution fusion | flops 1086323712 | bytes 19156992 | tf_op jit(solution)/shard_map/nd,kd->nk/dot_general | solution.py:22
  17.6 0.8 copy-done
  18.3 15.2 %all-reduce.1 = (f32[512]{0:T(512)S(1)}, f32[512]{0:T(512)S(1)}) all-reduce(f32[512]{0:T(512)S(1)} %get-tuple-element.5, f32[512]{0:T(512)S(1)} %get-tuple-element.6), channel_id=1, replica_groups=mesh['dp'=32,'cent'=8] {'cent'}, use_global_device_ids=true, to_apply=%region_5.0 | all-reduce | flops 1024 | bytes 8192 | tf_op jit(solution)/shard_map/pmax | solution.py:24
  33.5 7.6 %fusion.3 = (f32[512]{0:T(512)S(1)}, f32[512]{0:T(512)S(1)}) fusion(f32[512,4096]{1,0:T(8,128)} %get-tuple-element.17, f32[512]{0:T(512)S(1)} %get-tuple-element.9, f32[4096]{0:T(1024)S(1)} %fusion.4, f32[512]{0:T(512)S(1)} %get-tuple-element.10, f32[512,4096]{1,0:T(8,128)} %copy-done), kind=kLoop, calls=%fused_computation.11 | loop fusion | flops 16776192 | bytes 16801792 | tf_op jit(solution)/shard_map/reduce_sum | solution.py:26
  41.2 14.2 %all-reduce = (f32[512]{0:T(512)S(1)}, f32[512]{0:T(512)S(1)}) all-reduce(f32[512]{0:T(512)S(1)} %get-tuple-element.4, f32[512]{0:T(512)S(1)} %get-tuple-element.3), channel_id=1, replica_groups=mesh['dp'=32,'cent'=8] {'cent'}, use_global_device_ids=true, to_apply=%region_3.0 | all-reduce | flops 1024 | bytes 8192 | tf_op jit(solution)/shard_map/psum | solution.py:26
  55.4 8.7 %convert_reduce_fusion = (f32[4096]{0:T(1024)S(1)}, bf16[512,4096]{1,0:T(8,128)(2,1)S(1)}, f32[4096]{0:T(1024)S(1)}, bf16[512,4096]{1,0:T(8,128)(2,1)S(1)}) fusion(f32[512]{0:T(512)S(1)} %get-tuple-element.8, f32[512]{0:T(512)S(1)} %get-tuple-element.9, f32[4096]{0:T(1024)S(1)} %fusion.4, f32[512,4096]{1,0:T(8,128)} %get-tuple-element.17, ...), kind=kLoop, calls=%fused_computation | loop fusion | flops 29351936 | bytes 25223168 | tf_op jit(solution)/shard_map/reduce_sum | solution.py:29
  64.0 1.3 fusion.10
  65.3 3.4 convolution_add_fusion
  68.7 0.0 all-reduce.4.cloned.1.call-update
  68.8 159.1 %psum.31 = f32[4096]{0:T(1024)S(1)} all-reduce(f32[4096]{0:T(1024)S(1)} %add.33), channel_id=1, replica_groups=mesh['dp'=32,'cent'=8] {'dp'}, use_global_device_ids=true, to_apply=%region_11.0 | all-reduce | flops 4096 | bytes 32768 | tf_op jit(solution)/shard_map/psum | solution.py:32
  227.8 0.0 copy-start.3
  227.9 0.6 pad_maximum_fusion
  228.5 185.1 %all-reduce.4.cloned.1.call-done = f32[4096,256]{1,0:T(8,128)} async-done(((f32[4096,256]{1,0:T(8,128)}), f32[4096,256]{1,0:T(8,128)}) %all-reduce.4.cloned.1.call-update) | async-done | bytes 4194320 | tf_op jit(solution)/shard_map/psum | solution.py:32
  413.5 3.9 fusion.6
  417.5 0.0 copy-done.3
  (3 shorter events, 0.0 us)
Async XLA Ops:
  7.2 5.4 %copy-start.1 = (bf16[4096,256]{1,0:T(8,128)(2,1)S(1)}, bf16[4096,256]{1,0:T(8,128)(2,1)}, u32[]{:S(2)}) copy-start(bf16[4096,256]{1,0:T(8,128)(2,1)} %param.3) | copy-start | bytes 6291460
  7.2 5.4 %copy-start.2 = (bf16[1024,256]{1,0:T(8,128)(2,1)S(1)}, bf16[1024,256]{1,0:T(8,128)(2,1)}, u32[]{:S(2)}) copy-start(bf16[1024,256]{1,0:T(8,128)(2,1)} %param.2) | copy-start | bytes 1572868
  7.2 406.4 %all-reduce.4.cloned.1.call-start = ((), (), s32[]{:S(2)}) async-start(), calls=%async_computation | async-start | bytes 8388608 | tf_op jit(solution)/shard_map/psum | solution.py:32
  12.6 5.7 %copy-start = (f32[512,4096]{1,0:T(8,128)}, f32[512,4096]{1,0:T(8,128)S(1)}, u32[]{:S(2)}) copy-start(f32[512,4096]{1,0:T(8,128)S(1)} %fusion.12) | copy-start | bytes 25165828
  227.8 189.7 %copy-start.3 = (f32[4096]{0:T(1024)}, f32[4096]{0:T(1024)S(1)}, u32[]{:S(2)}) copy-start(f32[4096]{0:T(1024)S(1)} %psum.31) | copy-start | bytes 49156
Sparse Core Ops, SparseCore 0:
  68.9 344.6 all-reduce.3
where the time goes:
time: 425 us; the launch traced here: 424 us
  blocking collectives  188 us (44%)
  waiting for transfers between devices  185 us (44%)
  other arithmetic  23.2 us (5%)
  between operations  14.1 us (3%)
  matrix products  12.6 us (3%)
    psum x1, waiting for transfers between devices, body(): all_sums, all_counts = lax.psum((sums, counts), 'dp')  185 us
    psum x1, blocking collectives, body(): all_sums, all_counts = lax.psum((sums, counts), 'dp')  159 us
    pmax x1, blocking collectives, body(): top = lax.pmax(jnp.max(score, axis=1), 'cent')  15.2 us
    psum x1, blocking collectives, body(): total = lax.psum(jnp.sum(weights, axis=1), 'cent')  14.2 us
    reduce_sum x1, other arithmetic, body(): counts = counts + jnp.sum(resp.astype(jnp.float32), axis=0)  8.66 us
  transfers between devices with their start and end apart: 1, of which 1 were waited for; matrix products, arithmetic and copies ran while one was open for 0% of the time, Pallas kernels for 0%

commit v1 on v0

--- a/solution.py
+++ b/solution.py
@@ -1,3 +1,4 @@
+import functools
 import math
 import jax
 import jax.numpy as jnp
@@ -5,6 +6,14 @@
 from jax.sharding import PartitionSpec as P
 
 prior_mass = 0.5
+
+
+def quotas_supply_all(shard_in, named_axis):
+    r1 = jnp.sum(lax.all_gather(shard_in, named_axis), axis=0)
+    return r1
+
+
+patches_detail = functools.partial(quotas_supply_all, named_axis="cent")
 
 
 def body(points, centroids):
@@ -23,7 +32,7 @@
         score = 2.0 * dots - cnorm[None, :]
         top = lax.pmax(jnp.max(score, axis=1), "cent")
         weights = jnp.exp(score - top[:, None])
-        total = lax.psum(jnp.sum(weights, axis=1), "cent")
+        total = patches_detail(jnp.sum(weights, axis=1))
         resp = (weights / total[:, None]).astype(jnp.bfloat16)
         sums = sums + jnp.einsum("nk,nd->kd", resp, piece, preferred_element_type=jnp.float32)
         counts = counts + jnp.sum(resp.astype(jnp.float32), axis=0)

time: 425 us -> 439 us (1.033)
  blocking collectives: 188 us -> 203 us
    all_gather x0 -> x2, blocking collectives: none -> 28.7 us  [quotas_supply_all(): r1 = jnp.sum(lax.all_gather(shard_in, named_axis), axis=0)]
    psum x1 -> x0, blocking collectives: 14.2 us -> none  [body(): total = lax.psum(jnp.sum(weights, axis=1), 'cent')]
where the time goes in v1:
time: 439 us
  blocking collectives  203 us (46%)
  waiting for transfers between devices  186 us (42%)
  other arithmetic  23.3 us (5%)
  between operations  14.1 us (3%)
  matrix products  12.6 us (3%)
    psum x1, waiting for transfers between devices, body(): all_sums, all_counts = lax.psum((sums, counts), 'dp')  186 us
    psum x1, blocking collectives, body(): all_sums, all_counts = lax.psum((sums, counts), 'dp')  159 us
    all_gather x2, blocking collectives, quotas_supply_all(): r1 = jnp.sum(lax.all_gather(shard_in, named_axis), axis=0)  28.7 us
    pmax x1, blocking collectives, body(): top = lax.pmax(jnp.max(score, axis=1), 'cent')  15.2 us
  transfers between devices with their start and end apart: 1, of which 1 were waited for; matrix products, arithmetic and copies ran while one was open for 0% of the time, Pallas kernels for 0%

profile of v1, /device:TPU:64, one launch (start us, length us, event | category | flops | bytes accessed | tf_op | source)
XLA Modules:
  0.0 439.1 jit_solution(15582138189369916906)
XLA Ops:
  7.2 0.0 copy-start.1
  7.2 0.0 copy-start.2
  7.2 0.0 all-reduce.3.cloned.1.call-start
  7.2 2.4 fusion.4
  9.6 3.0 fusion.12
  12.6 0.0 copy-done.1
  12.6 0.0 copy-done.2
  12.6 0.0 copy-start
  12.6 4.9 %fusion.1 = (f32[512]{0:T(512)S(1)}, f32[512]{0:T(512)S(1)}, f32[512,4096]{1,0:T(8,128)}) fusion(f32[4096]{0:T(1024)S(1)} %fusion.4, f32[512,4096]{1,0:T(8,128)S(1)} %fusion.12, bf16[4096,256]{1,0:T(8,128)(2,1)S(1)} %copy-done.1, bf16[1024,256]{1,0:T(8,128)(2,1)S(1)} %copy-done.2), kind=kOutput, calls=%fused_computation.9 | convolution fusion | flops 1086323712 | bytes 19156992 | tf_op jit(solution)/shard_map/nd,kd->nk/dot_general | solution.py:31
  17.6 0.8 copy-done
  18.3 15.2 %all-reduce = (f32[512]{0:T(512)S(1)}, f32[512]{0:T(512)S(1)}) all-reduce(f32[512]{0:T(512)S(1)} %get-tuple-element.5, f32[512]{0:T(512)S(1)} %get-tuple-element.6), channel_id=1, replica_groups=mesh['dp'=32,'cent'=8] {'cent'}, use_global_device_ids=true, to_apply=%region_5.0 | all-reduce | flops 1024 | bytes 8192 | tf_op jit(solution)/shard_map/pmax | solution.py:33
  33.5 7.6 %fusion.3 = (f32[512]{0:T(512)S(1)}, f32[512]{0:T(512)S(1)}) fusion(f32[512,4096]{1,0:T(8,128)} %get-tuple-element.15, f32[512]{0:T(512)S(1)} %get-tuple-element.7, f32[4096]{0:T(1024)S(1)} %fusion.4, f32[512]{0:T(512)S(1)} %get-tuple-element.8, f32[512,4096]{1,0:T(8,128)} %copy-done), kind=kLoop, calls=%fused_computation.11 | loop fusion | flops 16776192 | bytes 16801792 | tf_op jit(solution)/shard_map/reduce_sum | solution.py:35
  41.2 14.3 %all-gather.3 = f32[8,1,512]{2,1,0:T(1,128)S(1)} all-gather(f32[1,1,512]{2,1,0:T(1,128)S(1)} %bitcast.7), channel_id=3, replica_groups=mesh['dp'=32,'cent'=8] {'cent'}, dimensions={0}, use_global_device_ids=true | all-gather | bytes 18432 | tf_op jit(solution)/shard_map/all_gather | solution.py:12
  55.4 14.4 %all-gather.2 = f32[8,1,512]{2,1,0:T(1,128)S(1)} all-gather(f32[1,1,512]{2,1,0:T(1,128)S(1)} %bitcast.6), channel_id=2, replica_groups=mesh['dp'=32,'cent'=8] {'cent'}, dimensions={0}, use_global_device_ids=true | all-gather | bytes 18432 | tf_op jit(solution)/shard_map/all_gather | solution.py:12
  69.9 8.7 %convert_reduce_fusion = (f32[4096]{0:T(1024)S(1)}, bf16[512,4096]{1,0:T(8,128)(2,1)S(1)}, f32[4096]{0:T(1024)S(1)}, bf16[512,4096]{1,0:T(8,128)(2,1)S(1)}) fusion(f32[512]{0:T(512)S(1)} %reduce_sum.57, f32[512]{0:T(512)S(1)} %get-tuple-element.7, f32[4096]{0:T(1024)S(1)} %fusion.4, f32[512,4096]{1,0:T(8,128)} %get-tuple-element.15, f32[512]{0:T(512)S(1)} %reduce_sum.55, ...), kind=kLoop, calls=%fused_computation | loop fusion | flops 29351936 | bytes 25223168 | tf_op jit(solution)/shard_map/reduce_sum | solution.py:38
  78.6 1.3 fusion.10
  79.9 3.4 convolution_add_fusion
  83.3 0.0 all-reduce.3.cloned.1.call-update
  83.3 158.8 %psum.15 = f32[4096]{0:T(1024)S(1)} all-reduce(f32[4096]{0:T(1024)S(1)} %add.29), channel_id=1, replica_groups=mesh['dp'=32,'cent'=8] {'dp'}, use_global_device_ids=true, to_apply=%region_11.0 | all-reduce | flops 4096 | bytes 32768 | tf_op jit(solution)/shard_map/psum | solution.py:41
  242.1 0.0 copy-start.3
  242.1 0.6 pad_maximum_fusion
  242.7 185.6 %all-reduce.3.cloned.1.call-done = f32[4096,256]{1,0:T(8,128)} async-done(((f32[4096,256]{1,0:T(8,128)}), f32[4096,256]{1,0:T(8,128)}) %all-reduce.3.cloned.1.call-update) | async-done | bytes 4194320 | tf_op jit(solution)/shard_map/psum | solution.py:41
  428.3 3.9 fusion.6
  432.3 0.0 copy-done.3
  (6 shorter events, 0.1 us)
Async XLA Ops:
  7.2 5.4 %copy-start.1 = (bf16[4096,256]{1,0:T(8,128)(2,1)S(1)}, bf16[4096,256]{1,0:T(8,128)(2,1)}, u32[]{:S(2)}) copy-start(bf16[4096,256]{1,0:T(8,128)(2,1)} %param.3) | copy-start | bytes 6291460
  7.2 5.4 %copy-start.2 = (bf16[1024,256]{1,0:T(8,128)(2,1)S(1)}, bf16[1024,256]{1,0:T(8,128)(2,1)}, u32[]{:S(2)}) copy-start(bf16[1024,256]{1,0:T(8,128)(2,1)} %param.2) | copy-start | bytes 1572868
  7.2 421.2 %all-reduce.3.cloned.1.call-start = ((), (), s32[]{:S(2)}) async-start(), calls=%async_computation | async-start | bytes 8388608 | tf_op jit(solution)/shard_map/psum | solution.py:41
  12.6 5.7 %copy-start = (f32[512,4096]{1,0:T(8,128)}, f32[512,4096]{1,0:T(8,128)S(1)}, u32[]{:S(2)}) copy-start(f32[512,4096]{1,0:T(8,128)S(1)} %fusion.12) | copy-start | bytes 25165828
  242.1 190.2 %copy-start.3 = (f32[4096]{0:T(1024)}, f32[4096]{0:T(1024)S(1)}, u32[]{:S(2)}) copy-start(f32[4096]{0:T(1024)S(1)} %psum.15) | copy-start | bytes 49156
Sparse Core Ops, SparseCore 0:
  83.4 344.8 all-reduce.2
